TPU v7x, 32 devices: a whole 2x2x4 slice. The times are simulated.
32 devices in a mesh: gx: 8 (over z, core), gy: 4 (over y, x).
Axes of the slice: x: 2, y: 2, z: 4, core: 2. Of those that a mesh axis runs over, the one named last changes fastest.
Arguments:
- tangent_e: float32 [3, 64, 64, 256], P(None, 'gx', 'gy'), may hold values from -6 to 6
- tangent_h: float32 [3, 64, 64, 256], P(None, 'gx', 'gy'), may hold values from -6 to 6
- forward_e: float32 [3, 64, 64, 4], P(None, 'gx', 'gy'), may hold values from -6 to 6
- forward_h: float32 [3, 64, 64, 4], P(None, 'gx', 'gy'), may hold values from -6 to 6
- class_map: int32 [64, 64, 4], P('gx', 'gy'), may hold values from 0 to 63
- material: int32 [64, 64, 4], P('gx', 'gy'), may hold values from 0 to 3
- permittivity: float32 [4], replicated, may hold values from 1 to 4
- contrast: float32 [4], replicated, may hold values from 0.5 to 2
- order_list: int32 [1024, 2], replicated, may hold values from -16 to 16
Outputs:
- new_tangent_e: float32 [3, 64, 64, 256], P(None, 'gx', 'gy')
- new_tangent_h: float32 [3, 64, 64, 256], P(None, 'gx', 'gy')
- order_sens: float32 [1024, 256], P(('gx', 'gy'))
Inputs may be any that keep to these rules, and one draw needn't show every extreme that they name: `class_map`: feature class of each cell, naming its tangent direction.
All inputs are finite; a program needn't handle non-finite values.
Results may differ from a plain program's by a relative error of at most 0.0003.
Values sent between devices are 32-bit elements; how exact they have to be, the bound alone decides.
A program may use at most 64 MiB of HBM per device.

v0:
```python
import math

import jax
import jax.numpy as jnp
from jax import lax
from jax.sharding import PartitionSpec as P

DIRS = 64
ORDERS = 1024
STEPS = 2


time_step = 0.5


def passed_along(block, axis, distance):
    devices = range(lax.axis_size(axis))
    route = [((i - distance) % len(devices), i) for i in devices]
    return lax.ppermute(block, axis, route)


def next_z(field, unit):
    return jnp.concatenate([field[..., unit:], jnp.zeros_like(field[..., :unit])], -1)


def prev_z(field, unit):
    return jnp.concatenate([jnp.zeros_like(field[..., :unit]), field[..., :-unit]], -1)


def after_x(comp, plane):
    return jnp.concatenate([comp[1:], plane[None]], 0)


def after_y(comp, plane):
    return jnp.concatenate([comp[:, 1:], plane[:, None]], 1)


def before_x(comp, plane):
    return jnp.concatenate([plane[None], comp[:-1]], 0)


def before_y(comp, plane):
    return jnp.concatenate([plane[:, None], comp[:, :-1]], 1)


def curl_forward(field, rim_x, rim_y, unit):
    field_x, field_y, field_z = (field[0], field[1], field[2])
    curl_x = after_y(field_z, rim_y[0]) - field_z - (next_z(field_y, unit) - field_y)
    curl_y = next_z(field_x, unit) - field_x - (after_x(field_z, rim_x[0]) - field_z)
    curl_z = after_x(field_y, rim_x[1]) - field_y - (after_y(field_x, rim_y[1]) - field_x)
    return jnp.stack([curl_x, curl_y, curl_z])


def curl_backward(field, rim_x, rim_y, unit):
    field_x, field_y, field_z = (field[0], field[1], field[2])
    curl_x = field_z - before_y(field_z, rim_y[0]) - (field_y - prev_z(field_y, unit))
    curl_y = field_x - prev_z(field_x, unit) - (field_z - before_x(field_z, rim_x[0]))
    curl_z = field_y - before_x(field_y, rim_x[1]) - (field_x - before_y(field_x, rim_y[1]))
    return jnp.stack([curl_x, curl_y, curl_z])


def cell_values(material, table):
    hits = (material[..., None] == jnp.arange(table.shape[0], dtype=jnp.int32)).astype(jnp.float32)
    return jnp.sum(hits * table, -1)


def advance(state, inverse, inverse_wide, coef, onehot):
    tangent_e, tangent_h, forward_e, forward_h = state
    rim_ex = passed_along(
        (
            jnp.stack([tangent_e[2, 0], tangent_e[1, 0]]),
            jnp.stack([forward_e[2, 0], forward_e[1, 0]]),
        ),
        "gx",
        -1,
    )
    rim_ey = passed_along(
        (
            jnp.stack([tangent_e[2, :, 0], tangent_e[0, :, 0]]),
            jnp.stack([forward_e[2, :, 0], forward_e[0, :, 0]]),
        ),
        "gy",
        -1,
    )
    forward_h = forward_h - time_step * curl_forward(forward_e, rim_ex[1], rim_ey[1], 1)
    tangent_h = tangent_h - time_step * curl_forward(tangent_e, rim_ex[0], rim_ey[0], DIRS)
    rim_hx = passed_along(
        (
            jnp.stack([tangent_h[2, -1], tangent_h[1, -1]]),
            jnp.stack([forward_h[2, -1], forward_h[1, -1]]),
        ),
        "gx",
        1,
    )
    rim_hy = passed_along(
        (
            jnp.stack([tangent_h[2, :, -1], tangent_h[0, :, -1]]),
            jnp.stack([forward_h[2, :, -1], forward_h[0, :, -1]]),
        ),
        "gy",
        1,
    )
    curl_fwd = curl_backward(forward_h, rim_hx[1], rim_hy[1], 1)
    forward_e = forward_e + inverse[None] * curl_fwd
    curl_tan = curl_backward(tangent_h, rim_hx[0], rim_hy[0], DIRS)
    source = ((coef[None] * curl_fwd)[..., None] * onehot[None]).reshape(tangent_e.shape)
    tangent_e = tangent_e + inverse_wide[None] * curl_tan - source
    return (tangent_e, tangent_h, forward_e, forward_h)


def local(
    tangent_e,
    tangent_h,
    forward_e,
    forward_h,
    class_map,
    material,
    permittivity,
    contrast,
    order_list,
):
    eps_cell = cell_values(material, permittivity)
    inverse = time_step / eps_cell
    coef = time_step * cell_values(material, contrast) / (eps_cell * eps_cell)
    inverse_wide = jnp.repeat(inverse, DIRS, axis=-1)
    onehot = (class_map[..., None] == jnp.arange(DIRS, dtype=jnp.int32)).astype(jnp.float32)
    state = (tangent_e, tangent_h, forward_e, forward_h)
    for step in range(STEPS):
        state = advance(state, inverse, inverse_wide, coef, onehot)
    tangent_e, tangent_h = (state[0], state[1])
    width_x = tangent_e.shape[1]
    width_y = tangent_e.shape[2]
    layers = tangent_e.shape[3] // DIRS
    count_x = lax.axis_size("gx")
    count_y = lax.axis_size("gy")
    total_x = width_x * count_x
    total_y = width_y * count_y
    top = tangent_e[0:2, :, :, (layers - 1) * DIRS :]
    top = jnp.transpose(top, (1, 2, 0, 3)).reshape(width_x * width_y, 2 * DIRS)
    xs = lax.axis_index("gx") * width_x + jnp.arange(width_x, dtype=jnp.int32)
    ys = lax.axis_index("gy") * width_y + jnp.arange(width_y, dtype=jnp.int32)
    factor = 2.0 * math.pi / (total_x * total_y)
    scale = 1.0 / math.sqrt(total_x * total_y)
    highest = lax.Precision.HIGHEST
    own_rows = ORDERS // (count_x * count_y)
    count = own_rows * lax.axis_size(("gx", "gy"))
    order_m = order_list[:, 0]
    order_n = order_list[:, 1]
    index = (
        order_m[:, None, None] * xs[None, :, None] * total_y
        + order_n[:, None, None] * ys[None, None, :] * total_x
    )
    index = jnp.mod(index, total_x * total_y).reshape(count, width_x * width_y)
    theta = index.astype(jnp.float32) * factor
    real = jnp.dot(jnp.cos(theta), top, precision=highest, preferred_element_type=jnp.float32)
    imag = -jnp.dot(jnp.sin(theta), top, precision=highest, preferred_element_type=jnp.float32)
    both = jnp.stack([real.reshape(count, 2, DIRS), imag.reshape(count, 2, DIRS)], 2)
    order_sens = lax.psum_scatter(
        both.reshape(count, 4 * DIRS) * scale, ("gx", "gy"), scatter_dimension=0, tiled=True
    )
    return (tangent_e, tangent_h, order_sens)


def solution(mesh):
    in_specs = (
        P(None, "gx", "gy", None),
        P(None, "gx", "gy", None),
        P(None, "gx", "gy", None),
        P(None, "gx", "gy", None),
        P("gx", "gy", None),
        P("gx", "gy", None),
        P(),
        P(),
        P(),
    )
    out_specs = (P(None, "gx", "gy", None), P(None, "gx", "gy", None), P(("gx", "gy"), None))
    return jax.shard_map(local, mesh=mesh, in_specs=in_specs, out_specs=out_specs, check_vma=False)
```

profile of v0, /device:TPU:0, one launch (start us, length us, event | category | flops | bytes accessed | tf_op | source)
XLA Modules:
  0.0 214.3 jit_solution(5413079492115071697)
XLA Ops:
  7.2 0.7 slice_bitcast_fusion.88
  8.0 4.5 %collective-permute-start.5 = (f32[2,16,4]{1,2,0:T(4,128)S(1)}, f32[2,16,4]{1,2,0:T(4,128)S(1)}, u32[]{:S(2)}, u32[]{:S(2)}) collective-permute-start(f32[2,16,4]{1,2,0:T(4,128)S(1)} %pad_maximum_fusion.10), channel_id=1, source_target_pairs={{4,0},{8,4},{12,8},{16,12},{20,16},{24,20},{28,24},{0,28},{5,1},{9... | collective-permute-start | bytes 1544 | tf_op jit(solution)/shard_map/ppermute | solution.py:19
  12.5 0.9 slice_bitcast_fusion.68
  13.4 0.6 pad_maximum_fusion.5
  14.0 2.4 %collective-permute-start = (f32[2,8,256]{2,0,1:T(2,128)}, f32[2,8,256]{2,0,1:T(2,128)}, u32[]{:S(2)}, u32[]{:S(2)}) collective-permute-start(f32[2,8,256]{2,0,1:T(2,128)} %pad_maximum_fusion.5), channel_id=1, source_target_pairs={{1,0},{2,1},{3,2},{0,3},{5,4},{6,5},{7,6},{4,7},{9,8},{10,9},{11,1... | collective-permute-start | bytes 49160 | tf_op jit(solution)/shard_map/ppermute | solution.py:19
  16.6 0.6 collective-permute-start.4
  17.2 0.7 slice_bitcast_fusion.40
  18.0 0.6 pad_maximum_fusion.1
  18.6 0.1 collective-permute-start.1
  18.8 0.7 copy-done.16
  19.5 0.6 copy-done.18
  20.3 0.1 copy.119
  20.4 0.7 slice_bitcast_fusion.20
  21.2 0.6 copy-done.17
  21.9 0.1 copy.135
  22.0 0.2 eq.48
  22.2 0.2 eq.49
  22.6 2.0 fusion.10
  24.8 0.2 broadcast_in_dim.2
  25.0 0.2 mul.215
  25.7 0.4 copy-done.7
  26.1 0.3 copy-done.6
  26.8 1.6 collective-permute-start.6
  28.4 2.9 %collective-permute-done.6 = f32[2,8,4]{1,2,0:T(4,128)S(1)} collective-permute-done((f32[2,8,4]{1,2,0:T(4,128)S(1)}, f32[2,8,4]{1,2,0:T(4,128)S(1)}, u32[]{:S(2)}, u32[]{:S(2)}) %collective-permute-start.6) | collective-permute-done | bytes 288 | tf_op jit(solution)/shard_map/ppermute | solution.py:19
  31.6 1.6 collective-permute-done.7
  33.5 0.6 slice_bitcast_fusion.50
  34.3 1.5 collective-permute-start.12
  35.8 0.6 pad_maximum_fusion.14
  36.4 0.2 copy.134
  36.6 0.5 mul.226
  37.0 0.5 mul.227
  37.5 0.4 collective-permute-done.12
  38.2 0.7 fusion.63
  39.0 0.6 copy-done.13
  39.7 0.6 copy-done.8
  40.8 1.4 collective-permute-start.14
  42.2 3.1 %collective-permute-done.14 = f32[2,8,4]{1,2,0:T(4,128)S(1)} collective-permute-done((f32[2,8,4]{1,2,0:T(4,128)S(1)}, f32[2,8,4]{1,2,0:T(4,128)S(1)}, u32[]{:S(2)}, u32[]{:S(2)}) %collective-permute-start.14) | collective-permute-done | bytes 288 | tf_op jit(solution)/shard_map/ppermute | solution.py:19
  45.5 1.5 collective-permute-done.15
  47.2 0.2 copy.151
  47.4 0.5 mul.236
  47.9 0.5 mul.237
  48.4 0.8 slice_bitcast_fusion.66
  49.2 0.7 fusion.60
  49.9 1.0 slice_bitcast_fusion.16
  51.0 0.9 copy-done.5
  52.0 0.9 copy-done.2
  53.1 0.6 collective-permute-start.2
  53.8 4.0 %collective-permute-done.2 = f32[2,8,256]{2,0,1:T(2,128)S(1)} collective-permute-done((f32[2,8,256]{2,0,1:T(2,128)S(1)}, f32[2,8,256]{2,0,1:T(2,128)S(1)}, u32[]{:S(2)}, u32[]{:S(2)}) %collective-permute-start.2) | collective-permute-done | bytes 16416 | tf_op jit(solution)/shard_map/ppermute | solution.py:19
  57.8 1.2 collective-permute-done.3
  59.0 0.2 fusion.17
  59.2 0.1 fusion.5
  59.4 2.4 %collective-permute-start.8 = (f32[2,8,256]{2,0,1:T(2,128)S(1)}, f32[2,8,256]{2,0,1:T(2,128)S(1)}, u32[]{:S(2)}, u32[]{:S(2)}) collective-permute-start(f32[2,8,256]{2,0,1:T(2,128)S(1)} %pad_maximum_fusion.7), channel_id=1, source_target_pairs={{1,0},{2,1},{3,2},{0,3},{5,4},{6,5},{7,6},{4,7},{9,8},{10,9},{11,1... | collective-permute-start | bytes 49160 | tf_op jit(solution)/shard_map/ppermute | solution.py:19
  62.0 1.9 collective-permute-done.8
  64.5 3.0 %collective-permute-start.10 = (f32[2,8,256]{2,0,1:T(2,128)S(1)}, f32[2,8,256]{2,0,1:T(2,128)S(1)}, u32[]{:S(2)}, u32[]{:S(2)}) collective-permute-start(f32[2,8,256]{2,0,1:T(2,128)S(1)} %pad_maximum_fusion.8), channel_id=1, source_target_pairs={{3,0},{0,1},{1,2},{2,3},{7,4},{4,5},{5,6},{6,7},{11,8},{8,9},{9,10... | collective-permute-start | bytes 49160 | tf_op jit(solution)/shard_map/ppermute | solution.py:19
  67.6 1.6 collective-permute-done.10
  69.2 3.5 %collective-permute-done.11 = f32[2,16,256]{2,1,0:T(8,128)S(1)} collective-permute-done((f32[2,16,256]{2,1,0:T(8,128)S(1)}, f32[2,16,256]{2,1,0:T(8,128)S(1)}, u32[]{:S(2)}, u32[]{:S(2)}) %collective-permute-start.11) | collective-permute-done | bytes 32800 | tf_op jit(solution)/shard_map/ppermute | solution.py:19
  72.8 0.2 fusion.27
  72.9 0.1 fusion.8
  73.3 0.1 reshape.259
  73.5 0.3 copy-done.4
  73.8 0.6 convolution_negate_fusion
  74.4 0.6 convolution_bitcast_fusion
  75.3 1.3 copy.159
  76.6 130.9 %reduce-scatter.4.cloned.1.call-done = f32[32,256]{1,0:T(8,128)} async-done(((f32[1024,256]{1,0:T(8,128)}), f32[32,256]{1,0:T(8,128)}) %reduce-scatter.4.cloned.1.call-update) | async-done | bytes 32784
  (170 shorter events, 5.6 us)
Async XLA Ops:
  7.2 9.3 %copy-start.3 = (f32[3,8,16,4]{2,3,1,0:T(4,128)S(1)}, f32[3,8,16,4]{2,3,1,0:T(4,128)}, u32[]{:S(2)}) copy-start(f32[3,8,16,4]{2,3,1,0:T(4,128)} %param.11) | copy-start | bytes 18436
  7.2 13.2 %copy-start = (f32[3,8,16,256]{3,2,1,0:T(8,128)S(1)}, f32[3,8,16,256]{3,2,1,0:T(8,128)}, u32[]{:S(2)}) copy-start(f32[3,8,16,256]{3,2,1,0:T(8,128)} %param.9) | copy-start | bytes 1179652
  7.2 200.3 %reduce-scatter.4.cloned.1.call-start = ((), (), s32[]{:S(2)}) async-start(), calls=%async_computation.1 | async-start | bytes 1081344
  8.0 17.4 %collective-permute-start.5 = (f32[2,16,4]{1,2,0:T(4,128)S(1)}, f32[2,16,4]{1,2,0:T(4,128)S(1)}, u32[]{:S(2)}, u32[]{:S(2)}) collective-permute-start(f32[2,16,4]{1,2,0:T(4,128)S(1)} %pad_maximum_fusion.10), channel_id=1, source_target_pairs={{4,0},{8,4},{12,8},{16,12},{20,16},{24,20},{28,24},{0,28},{5,1},{9... | collective-permute-start | bytes 1544 | tf_op jit(solution)/shard_map/ppermute | solution.py:19
  14.0 34.4 %collective-permute-start = (f32[2,8,256]{2,0,1:T(2,128)}, f32[2,8,256]{2,0,1:T(2,128)}, u32[]{:S(2)}, u32[]{:S(2)}) collective-permute-start(f32[2,8,256]{2,0,1:T(2,128)} %pad_maximum_fusion.5), channel_id=1, source_target_pairs={{1,0},{2,1},{3,2},{0,3},{5,4},{6,5},{7,6},{4,7},{9,8},{10,9},{11,1... | collective-permute-start | bytes 49160 | tf_op jit(solution)/shard_map/ppermute | solution.py:19
  16.6 8.5 %collective-permute-start.4 = (f32[2,8,4]{1,2,0:T(4,128)S(1)}, f32[2,8,4]{1,2,0:T(4,128)S(1)}, u32[]{:S(2)}, u32[]{:S(2)}) collective-permute-start(f32[2,8,4]{1,2,0:T(4,128)S(1)} %pad_maximum_fusion.9), channel_id=1, source_target_pairs={{1,0},{2,1},{3,2},{0,3},{5,4},{6,5},{7,6},{4,7},{9,8},{10,9},{11,1... | collective-permute-start | bytes 776 | tf_op jit(solution)/shard_map/ppermute | solution.py:19
  18.6 30.6 %collective-permute-start.1 = (f32[2,16,256]{2,1,0:T(8,128)}, f32[2,16,256]{2,1,0:T(8,128)}, u32[]{:S(2)}, u32[]{:S(2)}) collective-permute-start(f32[2,16,256]{2,1,0:T(8,128)} %pad_maximum_fusion.1), channel_id=1, source_target_pairs={{4,0},{8,4},{12,8},{16,12},{20,16},{24,20},{28,24},{0,28},{5,1},{9... | collective-permute-start | bytes 98312 | tf_op jit(solution)/shard_map/ppermute | solution.py:19
  18.8 0.7 copy-start.16
  19.5 0.7 copy-start.18
  19.5 0.7 copy-start.19
  21.1 0.7 copy-start.17
  21.1 0.7 copy-start.15
  25.5 0.6 copy-start.7
  25.6 0.8 copy-start.6
  25.7 0.7 copy-start.9
  25.7 0.8 copy-start.11
  26.8 4.6 %collective-permute-start.6 = (f32[2,8,4]{1,2,0:T(4,128)S(1)}, f32[2,8,4]{1,2,0:T(4,128)S(1)}, u32[]{:S(2)}, u32[]{:S(2)}) collective-permute-start(f32[2,8,4]{1,2,0:T(4,128)S(1)} %pad_maximum_fusion.11), channel_id=1, source_target_pairs={{3,0},{0,1},{1,2},{2,3},{7,4},{4,5},{5,6},{6,7},{11,8},{8,9},{9,10... | collective-permute-start | bytes 776 | tf_op jit(solution)/shard_map/ppermute | solution.py:19
  28.3 4.8 %collective-permute-start.7 = (f32[2,16,4]{1,2,0:T(4,128)S(1)}, f32[2,16,4]{1,2,0:T(4,128)S(1)}, u32[]{:S(2)}, u32[]{:S(2)}) collective-permute-start(f32[2,16,4]{1,2,0:T(4,128)S(1)} %pad_maximum_fusion.12), channel_id=1, source_target_pairs={{28,0},{0,4},{4,8},{8,12},{12,16},{16,20},{20,24},{24,28},{29,1},{... | collective-permute-start | bytes 1544 | tf_op jit(solution)/shard_map/ppermute | solution.py:19
  34.3 3.6 %collective-permute-start.12 = (f32[2,8,4]{1,2,0:T(4,128)S(1)}, f32[2,8,4]{1,2,0:T(4,128)S(1)}, u32[]{:S(2)}, u32[]{:S(2)}) collective-permute-start(f32[2,8,4]{1,2,0:T(4,128)S(1)} %pad_maximum_fusion.13), channel_id=1, source_target_pairs={{1,0},{2,1},{3,2},{0,3},{5,4},{6,5},{7,6},{4,7},{9,8},{10,9},{11,1... | collective-permute-start | bytes 776 | tf_op jit(solution)/shard_map/ppermute | solution.py:19
  36.4 1.8 collective-permute-start.13
  38.0 0.8 copy-start.14
  38.9 0.7 copy-start.13
  39.7 0.7 copy-start.8
  39.7 0.7 copy-start.10
  39.7 0.7 copy-start.12
  40.8 4.5 %collective-permute-start.14 = (f32[2,8,4]{1,2,0:T(4,128)S(1)}, f32[2,8,4]{1,2,0:T(4,128)S(1)}, u32[]{:S(2)}, u32[]{:S(2)}) collective-permute-start(f32[2,8,4]{1,2,0:T(4,128)S(1)} %pad_maximum_fusion.15), channel_id=1, source_target_pairs={{3,0},{0,1},{1,2},{2,3},{7,4},{4,5},{5,6},{6,7},{11,8},{8,9},{9,10... | collective-permute-start | bytes 776 | tf_op jit(solution)/shard_map/ppermute | solution.py:19
  42.2 4.8 %collective-permute-start.15 = (f32[2,16,4]{1,2,0:T(4,128)S(1)}, f32[2,16,4]{1,2,0:T(4,128)S(1)}, u32[]{:S(2)}, u32[]{:S(2)}) collective-permute-start(f32[2,16,4]{1,2,0:T(4,128)S(1)} %pad_maximum_fusion.16), channel_id=1, source_target_pairs={{28,0},{0,4},{4,8},{8,12},{12,16},{16,20},{20,24},{24,28},{29,1},{... | collective-permute-start | bytes 1544 | tf_op jit(solution)/shard_map/ppermute | solution.py:19
  51.0 0.9 copy-start.5
  51.9 1.0 copy-start.2
  53.1 4.7 %collective-permute-start.2 = (f32[2,8,256]{2,0,1:T(2,128)S(1)}, f32[2,8,256]{2,0,1:T(2,128)S(1)}, u32[]{:S(2)}, u32[]{:S(2)}) collective-permute-start(f32[2,8,256]{2,0,1:T(2,128)S(1)} %pad_maximum_fusion.6), channel_id=1, source_target_pairs={{3,0},{0,1},{1,2},{2,3},{7,4},{4,5},{5,6},{6,7},{11,8},{8,9},{9,10... | collective-permute-start | bytes 49160 | tf_op jit(solution)/shard_map/ppermute | solution.py:19
  53.7 5.2 %collective-permute-start.3 = (f32[2,16,256]{2,1,0:T(8,128)S(1)}, f32[2,16,256]{2,1,0:T(8,128)S(1)}, u32[]{:S(2)}, u32[]{:S(2)}) collective-permute-start(f32[2,16,256]{2,1,0:T(8,128)S(1)} %pad_maximum_fusion.2), channel_id=1, source_target_pairs={{28,0},{0,4},{4,8},{8,12},{12,16},{16,20},{20,24},{24,28},{29,1},{... | collective-permute-start | bytes 98312 | tf_op jit(solution)/shard_map/ppermute | solution.py:19
  59.4 4.5 %collective-permute-start.8 = (f32[2,8,256]{2,0,1:T(2,128)S(1)}, f32[2,8,256]{2,0,1:T(2,128)S(1)}, u32[]{:S(2)}, u32[]{:S(2)}) collective-permute-start(f32[2,8,256]{2,0,1:T(2,128)S(1)} %pad_maximum_fusion.7), channel_id=1, source_target_pairs={{1,0},{2,1},{3,2},{0,3},{5,4},{6,5},{7,6},{4,7},{9,8},{10,9},{11,1... | collective-permute-start | bytes 49160 | tf_op jit(solution)/shard_map/ppermute | solution.py:19
  61.9 2.0 collective-permute-start.9
  64.4 8.4 %copy-start.1 = (f32[3,8,16,256]{3,2,1,0:T(8,128)}, f32[3,8,16,256]{3,2,1,0:T(8,128)S(1)}, u32[]{:S(2)}) copy-start(f32[3,8,16,256]{3,2,1,0:T(8,128)S(1)} %fusion.6) | copy-start | bytes 1179652
  64.5 4.7 %collective-permute-start.10 = (f32[2,8,256]{2,0,1:T(2,128)S(1)}, f32[2,8,256]{2,0,1:T(2,128)S(1)}, u32[]{:S(2)}, u32[]{:S(2)}) collective-permute-start(f32[2,8,256]{2,0,1:T(2,128)S(1)} %pad_maximum_fusion.8), channel_id=1, source_target_pairs={{3,0},{0,1},{1,2},{2,3},{7,4},{4,5},{5,6},{6,7},{11,8},{8,9},{9,10... | collective-permute-start | bytes 49160 | tf_op jit(solution)/shard_map/ppermute | solution.py:19
  67.5 5.2 %collective-permute-start.11 = (f32[2,16,256]{2,1,0:T(8,128)S(1)}, f32[2,16,256]{2,1,0:T(8,128)S(1)}, u32[]{:S(2)}, u32[]{:S(2)}) collective-permute-start(f32[2,16,256]{2,1,0:T(8,128)S(1)} %pad_maximum_fusion.4), channel_id=1, source_target_pairs={{28,0},{0,4},{4,8},{8,12},{12,16},{16,20},{20,24},{24,28},{29,1},{... | collective-permute-start | bytes 98312 | tf_op jit(solution)/shard_map/ppermute | solution.py:19
  73.1 0.7 copy-start.4
Sparse Core Ops, SparseCore 0:
  76.7 130.7 reduce-scatter.3
where the time goes:
time: 216 us; the launch traced here: 214 us
  waiting for transfers between devices  153 us (71%)
  local copies, waits for them, and re-layouts  20.1 us (9%)
  starting transfers between devices  18.4 us (9%)
  between operations  14.8 us (7%)
  other arithmetic  7.21 us (3%)
    unnamed x2, waiting for transfers between devices  131 us
    ppermute x16, waiting for transfers between devices, passed_along(): return lax.ppermute(block, axis, route)  21.7 us
    ppermute x16, starting transfers between devices, passed_along(): return lax.ppermute(block, axis, route)  18.3 us
    unnamed x43, local copies, waits for them, and re-layouts  7.51 us
  transfers between devices with their start and end apart: 17, of which 11 were waited for; matrix products, arithmetic and copies ran while one was open for 7% of the time, Pallas kernels for 0%

commit v1 on v0

v1 whole, which is shorter than its diff:
```python
import functools
import math

import jax
import jax.numpy as jnp
from jax import lax
from jax.experimental import pallas as pl
from jax.experimental.pallas import tpu as pltpu
from jax.sharding import PartitionSpec as P

DIRS = 64
STEPS = 2
LAYERS = 4
WIDE = LAYERS * DIRS
HALF = WIDE // 2
HIGHEST = lax.Precision.HIGHEST
time_step = 0.5


def lanes_of(shape):
    return lax.broadcasted_iota(jnp.int32, shape, len(shape) - 1)


def sublanes_of(shape):
    return lax.broadcasted_iota(jnp.int32, shape, len(shape) - 2)


def next_z(f):
    return jnp.where(lanes_of(f.shape) < WIDE - DIRS, pltpu.roll(f, WIDE - DIRS, f.ndim - 1), 0.0)


def prev_z(f):
    return jnp.where(lanes_of(f.shape) >= DIRS, pltpu.roll(f, DIRS, f.ndim - 1), 0.0)


def after_rows(f, row):
    n = f.shape[-2]
    return jnp.where(sublanes_of(f.shape) == n - 1, row, pltpu.roll(f, n - 1, f.ndim - 2))


def before_rows(f, row):
    return jnp.where(sublanes_of(f.shape) == 0, row, pltpu.roll(f, 1, f.ndim - 2))


def after_x(f, plane):
    return jnp.concatenate([f[1:], plane[None]], 0)


def before_x(f, plane):
    return jnp.concatenate([plane[None], f[:-1]], 0)


def packed(v):
    low, high = v[..., :HALF], v[..., HALF:]
    return jnp.where(lanes_of(low.shape) % DIRS < DIRS // 2, low, high)


def unpacked(v):
    near = lanes_of(v.shape) % DIRS < DIRS // 2
    axis = v.ndim - 1
    low = jnp.where(near, v, pltpu.roll(v, DIRS // 2, axis))
    high = jnp.where(near, pltpu.roll(v, HALF - DIRS // 2, axis), v)
    return jnp.concatenate([low, high], axis)


def put(buf, at, tangent, forward):
    n = len(tangent)
    for k in range(n):
        buf[at, 2 * k] = tangent[k][:, :HALF]
        buf[at, 2 * k + 1] = tangent[k][:, HALF:]
        buf[at, 2 * n + k] = packed(forward[k])


def take(buf, at, n):
    tangent = [jnp.concatenate([buf[at, 2 * k], buf[at, 2 * k + 1]], -1) for k in range(n)]
    forward = [unpacked(buf[at, 2 * n + k]) for k in range(n)]
    return (tangent, forward)


def sine(turn):
    u = turn * (2.0 * math.pi)
    s = u * u
    poly = -1.0 / 39916800.0
    for c in (1.0 / 362880.0, -1.0 / 5040.0, 1.0 / 120.0, -1.0 / 6.0):
        poly = poly * s + c
    return u + u * (s * poly)


def half_step_h(e, h, rim):
    ex, ey, ez = e
    hx, hy, hz = h
    xp, yp, xm, ym, cx, cy = rim
    new = (
        hx - time_step * ((after_rows(ez, yp[1][:, None, :]) - ez) - (next_z(ey) - ey)),
        hy - time_step * ((next_z(ex) - ex) - (after_x(ez, xp[1]) - ez)),
        hz - time_step * ((after_x(ey, xp[0]) - ey) - (after_rows(ex, yp[0][:, None, :]) - ex)),
    )
    x_y = xm[3] - time_step * ((next_z(xm[0]) - xm[0]) - (ez[0] - xm[2]))
    x_z = xm[4] - time_step * ((ey[0] - xm[1]) - (after_rows(xm[0], cx) - xm[0]))
    y_x = ym[3] - time_step * ((ez[:, 0, :] - ym[2]) - (next_z(ym[1]) - ym[1]))
    y_z = ym[4] - time_step * ((after_rows(ym[1], cy) - ym[1]) - (ex[:, 0, :] - ym[0]))
    return new, (x_y, x_z, y_x, y_z)


def curl_b(h, rim):
    hx, hy, hz = h
    x_y, x_z, y_x, y_z = rim
    return (
        (hz - before_rows(hz, y_z[:, None, :])) - (hy - prev_z(hy)),
        (hx - prev_z(hx)) - (hz - before_x(hz, x_z)),
        (hy - before_x(hy, x_y)) - (hx - before_rows(hx, y_x[:, None, :])),
    )


def widened(ref, lead):
    ny = ref.shape[-1]
    flat = LAYERS * ny
    total = 0.0
    for z in range(LAYERS):
        part = ref[..., z, :].reshape(lead, ny).astype(jnp.float32)
        place = (
            lax.broadcasted_iota(jnp.int32, (ny, flat), 1)
            == lax.broadcasted_iota(jnp.int32, (ny, flat), 0) + z * ny
        ).astype(jnp.float32)
        total = total + jnp.dot(part, place, precision=HIGHEST, preferred_element_type=jnp.float32)
    rows = jnp.broadcast_to(total[:, None, :], (lead, ny, flat))
    rows = jnp.where(lanes_of(rows.shape) % ny == sublanes_of(rows.shape), rows, 0.0)
    spread = (
        lax.broadcasted_iota(jnp.int32, (flat, WIDE), 0) // ny
        == lax.broadcasted_iota(jnp.int32, (flat, WIDE), 1) // DIRS
    ).astype(jnp.float32)
    wide = jnp.dot(
        rows.reshape(lead * ny, flat), spread, precision=HIGHEST, preferred_element_type=jnp.float32
    )
    return wide.reshape(lead, ny, WIDE)


def kernel(
    nx, ny, own,
    te, th, fe, fh, classes, material, permittivity, contrast, orders,
    out_e, out_h, out_s,
    s_xm, r_xm, s_xp, r_xp, s_ym, r_ym, s_yp, r_yp, s_cx, r_cx, s_cy, r_cy,
    gathered, partial, arrived, table_c, table_s,
    rim_send, rim_recv, g_send, g_recv, p_send, p_recv,
):
    wx, wy = te.shape[1], te.shape[2]
    i, j = lax.axis_index("gx"), lax.axis_index("gy")
    up, down = lax.rem(i + 1, nx), lax.rem(i + nx - 1, nx)
    right, left = lax.rem(j + 1, ny), lax.rem(j + ny - 1, ny)
    barrier = pltpu.get_barrier_semaphore()
    peers = [(lax.rem(i + d, nx), j) for d in range(1, nx)]
    peers += [(i, lax.rem(j + d, ny)) for d in range(1, ny)]
    peers += [(up, left), (down, right)]
    for peer in peers:
        pl.semaphore_signal(barrier, inc=1, device_id=peer, device_id_type=pl.DeviceIdType.MESH)

    def copy(src, dst, send, recv, device):
        return pltpu.make_async_remote_copy(
            src_ref=src, dst_ref=dst, send_sem=send, recv_sem=recv,
            device_id=device, device_id_type=pl.DeviceIdType.MESH,
        )

    def exchange(step, e, h, fe, fh):
        put(s_xm, step, [f[wx - 1] for f in (e[0], e[1], e[2], h[1], h[2])],
            [f[wx - 1] for f in (fe[0], fe[1], fe[2], fh[1], fh[2])])
        put(s_xp, step, [e[1][0], e[2][0]], [fe[1][0], fe[2][0]])
        put(s_ym, step, [f[:, wy - 1, :] for f in (e[0], e[1], e[2], h[0], h[2])],
            [f[:, wy - 1, :] for f in (fe[0], fe[1], fe[2], fh[0], fh[2])])
        put(s_yp, step, [e[0][:, 0, :], e[2][:, 0, :]], [fe[0][:, 0, :], fe[2][:, 0, :]])
        put(s_cx, step, [e[0][wx - 1, 0:1, :]], [fe[0][wx - 1, 0:1, :]])
        put(s_cy, step, [e[1][0, wy - 1:wy, :]], [fe[1][0, wy - 1:wy, :]])
        plan = (
            (s_xm, r_xm, (up, j)), (s_ym, r_ym, (i, right)), (s_xp, r_xp, (down, j)),
            (s_yp, r_yp, (i, left)), (s_cx, r_cx, (up, left)), (s_cy, r_cy, (down, right)),
        )
        if step == 0:
            pl.semaphore_wait(barrier, len(peers))
        copies = [
            copy(s.at[step], r.at[step], rim_send.at[step, k], rim_recv.at[step, k], device)
            for k, (s, r, device) in enumerate(plan)
        ]
        for c in copies:
            c.start()
        return copies

    e = [te[c] for c in range(3)]
    h = [th[c] for c in range(3)]
    wide_e = widened(fe, 3 * wx)
    wide_h = widened(fh, 3 * wx)
    fwd_e = [wide_e[c * wx:(c + 1) * wx] for c in range(3)]
    fwd_h = [wide_h[c * wx:(c + 1) * wx] for c in range(3)]
    waiting = exchange(0, e, h, fwd_e, fwd_h)

    kind = widened(material, wx)
    eps = jnp.zeros_like(kind)
    slope = jnp.zeros_like(kind)
    for k in range(permittivity.shape[0]):
        eps = jnp.where(kind == float(k), permittivity[k], eps)
        slope = jnp.where(kind == float(k), contrast[k], slope)
    inverse = time_step / eps
    coef = time_step * slope / (eps * eps)
    hot = widened(classes, wx) == (lanes_of(kind.shape) % DIRS).astype(jnp.float32)
    coef = jnp.where(hot, coef, 0.0)

    rows, cells = nx * own, ny * wx * wy
    count = orders.shape[1]
    row = lax.broadcasted_iota(jnp.int32, (rows, 1), 0)
    target = (row // own) * (ny * own) + j * own + row % own
    pick = (lax.broadcasted_iota(jnp.int32, (rows, count), 1) == target).astype(jnp.float32)
    pair = lax.dot_general(
        pick.astype(jnp.bfloat16), orders[...].astype(jnp.float32).astype(jnp.bfloat16),
        (((1,), (1,)), ((), ())), preferred_element_type=jnp.float32,
    )
    cell = lax.broadcasted_iota(jnp.int32, (1, cells), 1)
    all_x, all_y = nx * wx, ny * wy
    x_at = ((i * wx + (cell // wy) % wx) * all_y).astype(jnp.float32)
    y_at = (((cell // (wx * wy)) * wy + cell % wy) * all_x).astype(jnp.float32)
    index = pair[:, 0:1] * x_at + pair[:, 1:2] * y_at
    index = index - float(all_x * all_y) * jnp.round(index * (1.0 / (all_x * all_y)))
    turn = index * (1.0 / (all_x * all_y))
    table_c[...] = sine(0.25 - jnp.abs(turn))
    table_s[...] = sine(jnp.where(turn > 0.25, 0.5 - turn, jnp.where(turn < -0.25, -0.5 - turn, turn)))

    for step in range(STEPS):
        for c in waiting:
            c.wait()
        xm, ym = take(r_xm, step, 5), take(r_ym, step, 5)
        xp, yp = take(r_xp, step, 2), take(r_yp, step, 2)
        cx, cy = take(r_cx, step, 1), take(r_cy, step, 1)
        fwd_h, rim = half_step_h(fwd_e, fwd_h, (xp[1], yp[1], xm[1], ym[1], cx[1][0], cy[1][0]))
        fwd_c = curl_b(fwd_h, rim)
        fwd_e = [fwd_e[c] + inverse * fwd_c[c] for c in range(3)]
        h, rim = half_step_h(e, h, (xp[0], yp[0], xm[0], ym[0], cx[0][0], cy[0][0]))
        tan_c = curl_b(h, rim)
        e = [e[c] + inverse * tan_c[c] - coef * fwd_c[c] for c in range(3)]
        if step < STEPS - 1:
            waiting = exchange(step + 1, e, h, fwd_e, fwd_h)

    top_x, top_y = e[0][:, :, HALF:], e[1][:, :, HALF:]
    top = jnp.where(lanes_of(top_x.shape) < DIRS, pltpu.roll(top_x, DIRS, 2), top_y)
    gathered[j] = top.reshape(wx * wy, 2 * DIRS)
    copies = [
        copy(gathered.at[j], gathered.at[j], g_send.at[d], g_recv.at[d], (i, lax.rem(j + d, ny)))
        for d in range(1, ny)
    ]
    for c in copies:
        c.start()
    for c in range(3):
        out_e[c] = e[c]
        out_h[c] = h[c]
    for c in copies:
        c.wait()
    every = gathered[...].reshape(cells, 2 * DIRS)
    real = jnp.dot(table_c[...], every, precision=HIGHEST, preferred_element_type=jnp.float32)
    imag = jnp.dot(table_s[...], every, precision=HIGHEST, preferred_element_type=jnp.float32)
    for k in range(nx):
        partial[k, 0] = real[k * own:(k + 1) * own]
        partial[k, 1] = imag[k * own:(k + 1) * own]
    copies = []
    for d in range(1, nx):
        peer = lax.rem(i + d, nx)
        copies.append(copy(partial.at[peer], arrived.at[d - 1], p_send.at[d], p_recv.at[d], (peer, j)))
    for c in copies:
        c.start()
    total = partial[i]
    for c in copies:
        c.wait()
    for d in range(nx - 1):
        total = total + arrived[d]
    scale = 1.0 / math.sqrt(all_x * all_y)
    re, im = total[0] * scale, total[1] * -scale
    low = lanes_of(re.shape) < DIRS
    out_s[:, :2 * DIRS] = jnp.where(low, re, pltpu.roll(im, DIRS, 1))
    out_s[:, 2 * DIRS:] = jnp.where(low, pltpu.roll(re, DIRS, 1), im)


def local(nx, ny, te, th, fe, fh, classes, material, permittivity, contrast, orders):
    wx, wy = te.shape[1], te.shape[2]
    own = orders.shape[0] // (nx * ny)
    rows, cells = nx * own, ny * wx * wy
    f32 = jnp.float32
    vmem = pl.BlockSpec(memory_space=pltpu.VMEM)
    smem = pl.BlockSpec(memory_space=pltpu.SMEM)

    def two(*shape):
        return [pltpu.VMEM((STEPS,) + shape, f32)] * 2

    return pl.pallas_call(
        functools.partial(kernel, nx, ny, own),
        out_shape=(
            jax.ShapeDtypeStruct(te.shape, f32),
            jax.ShapeDtypeStruct(th.shape, f32),
            jax.ShapeDtypeStruct((own, 4 * DIRS), f32),
        ),
        in_specs=[vmem] * 6 + [smem] * 2 + [vmem],
        out_specs=(vmem, vmem, vmem),
        scratch_shapes=[
            *two(15, wy, HALF), *two(6, wy, HALF), *two(15, wx, HALF), *two(6, wx, HALF),
            *two(3, 1, HALF), *two(3, 1, HALF),
            pltpu.VMEM((ny, wx * wy, 2 * DIRS), f32),
            pltpu.VMEM((nx, 2, own, 2 * DIRS), f32),
            pltpu.VMEM((nx - 1, 2, own, 2 * DIRS), f32),
            pltpu.VMEM((rows, cells), f32),
            pltpu.VMEM((rows, cells), f32),
            pltpu.SemaphoreType.DMA((STEPS, 6)), pltpu.SemaphoreType.DMA((STEPS, 6)),
            pltpu.SemaphoreType.DMA((ny,)), pltpu.SemaphoreType.DMA((ny,)),
            pltpu.SemaphoreType.DMA((nx,)), pltpu.SemaphoreType.DMA((nx,)),
        ],
        compiler_params=pltpu.CompilerParams(
            collective_id=0, has_side_effects=True, vmem_limit_bytes=40 * 1024 * 1024
        ),
        name="slab",
    )(
        te, th, jnp.transpose(fe, (0, 1, 3, 2)), jnp.transpose(fh, (0, 1, 3, 2)),
        jnp.transpose(classes, (0, 2, 1)), jnp.transpose(material, (0, 2, 1)),
        permittivity, contrast, jnp.transpose(orders),
    )


def solution(mesh):
    in_specs = (
        P(None, "gx", "gy", None),
        P(None, "gx", "gy", None),
        P(None, "gx", "gy", None),
        P(None, "gx", "gy", None),
        P("gx", "gy", None),
        P("gx", "gy", None),
        P(),
        P(),
        P(),
    )
    out_specs = (P(None, "gx", "gy", None), P(None, "gx", "gy", None), P(("gx", "gy"), None))
    body = functools.partial(local, mesh.shape["gx"], mesh.shape["gy"])
    return jax.shard_map(body, mesh=mesh, in_specs=in_specs, out_specs=out_specs, check_vma=False)
```

time: 216 us -> 37 us (0.17)
  the two profiles are of different devices: /device:TPU:0 before, /device:TPU:1 now
where the time goes in v1:
time: 37 us; the launch traced here: 36.5 us
  Pallas kernels  28 us (76%)
  local copies, waits for them, and re-layouts  7.81 us (21%)
  between operations  0.67 us (2%)
    pallas_call x1, Pallas kernels, local(): pl.pallas_call(functools.partial(kernel, nx, ny, own), out_shape=(jax.Sha...  28 us
    unnamed x21, local copies, waits for them, and re-layouts  7.81 us

profile of v1, /device:TPU:1, one launch (start us, length us, event | category | flops | bytes accessed | tf_op | source)
XLA Modules:
  0.0 36.5 jit_solution(16856319156178385478)
XLA Ops:
  0.6 0.0 copy-start.6
  0.6 0.0 copy-start.7
  0.7 0.0 copy-start.8
  0.7 0.7 %copy-done.6 = s32[1024,2]{0,1:T(2,128)S(1)} copy-done((s32[1024,2]{0,1:T(2,128)S(1)}, s32[1024,2]{0,1:T(2,128)}, u32[]{:S(2)}) %copy-start.6) | copy-done | bytes 8216
  1.3 0.0 copy-done.7
  1.3 0.0 copy-done.8
  1.3 0.0 copy-start
  1.3 1.0 %copy-done = f32[3,8,16,256]{3,2,1,0:T(8,128)S(1)} copy-done((f32[3,8,16,256]{3,2,1,0:T(8,128)S(1)}, f32[3,8,16,256]{3,2,1,0:T(8,128)}, u32[]{:S(2)}) %copy-start) | copy-done | bytes 393240
  2.3 0.0 copy-start.1
  2.3 1.0 %copy-done.1 = f32[3,8,16,256]{3,2,1,0:T(8,128)S(1)} copy-done((f32[3,8,16,256]{3,2,1,0:T(8,128)S(1)}, f32[3,8,16,256]{3,2,1,0:T(8,128)}, u32[]{:S(2)}) %copy-start.1) | copy-done | bytes 393240
  3.3 0.0 copy-start.2
  3.3 0.8 %copy-done.2 = f32[3,8,16,4]{2,3,1,0:T(4,128)S(1)} copy-done((f32[3,8,16,4]{2,3,1,0:T(4,128)S(1)}, f32[3,8,16,4]{2,3,1,0:T(4,128)}, u32[]{:S(2)}) %copy-start.2) | copy-done | bytes 6168
  4.1 0.0 copy-start.3
  4.1 0.8 %copy-done.3 = f32[3,8,16,4]{2,3,1,0:T(4,128)S(1)} copy-done((f32[3,8,16,4]{2,3,1,0:T(4,128)S(1)}, f32[3,8,16,4]{2,3,1,0:T(4,128)}, u32[]{:S(2)}) %copy-start.3) | copy-done | bytes 6168
  4.9 0.0 copy-start.4
  4.9 0.7 %copy-done.4 = s32[8,16,4]{1,2,0:T(4,128)S(1)} copy-done((s32[8,16,4]{1,2,0:T(4,128)S(1)}, s32[8,16,4]{1,2,0:T(4,128)}, u32[]{:S(2)}) %copy-start.4) | copy-done | bytes 2072
  5.6 0.0 copy-start.5
  5.6 0.7 %copy-done.5 = s32[8,16,4]{1,2,0:T(4,128)S(1)} copy-done((s32[8,16,4]{1,2,0:T(4,128)S(1)}, s32[8,16,4]{1,2,0:T(4,128)}, u32[]{:S(2)}) %copy-start.5) | copy-done | bytes 2072
  6.4 28.0 %slab.1 = (f32[3,8,16,256]{3,2,1,0:T(8,128)S(1)}, f32[3,8,16,256]{3,2,1,0:T(8,128)S(1)}, f32[32,256]{1,0:T(8,128)S(1)}) custom-call(f32[3,8,16,256]{3,2,1,0:T(8,128)S(1)} %copy-done, f32[3,8,16,256]{3,2,1,0:T(8,128)S(1)} %copy-done.1, f32[3,8,4,16]{3,2,1,0:T(4,128)S(1)} %bitcast.5, f32[3,8,4,16]{3,2,1,0:T(4,128)S(1)} %bitcast.6, s32[8,4,16]{2,1,0:T(4,128)S(1)} %bitcast.7, ...), custom_call_target="tpu_custom_call" | custom-call | tf_op jit(solution)/shard_map/slab/pallas_call | solution.py:288
  34.4 0.7 %copy.15 = f32[3,8,16,256]{3,2,1,0:T(8,128)} copy(f32[3,8,16,256]{3,2,1,0:T(8,128)S(1)} %get-tuple-element.6) | data formatting | bytes 786432
  35.1 0.7 %copy.16 = f32[3,8,16,256]{3,2,1,0:T(8,128)} copy(f32[3,8,16,256]{3,2,1,0:T(8,128)S(1)} %get-tuple-element.7) | data formatting | bytes 786432
  35.9 0.6 %copy.17 = f32[32,256]{1,0:T(8,128)} copy(f32[32,256]{1,0:T(8,128)S(1)} %get-tuple-element.8) | data formatting | bytes 65536
Async XLA Ops:
  0.6 0.7 %copy-start.6 = (s32[1024,2]{0,1:T(2,128)S(1)}, s32[1024,2]{0,1:T(2,128)}, u32[]{:S(2)}) copy-start(s32[1024,2]{0,1:T(2,128)} %param.17) | copy-start | bytes 24580
  0.6 0.7 %copy-start.7 = (f32[4]{0:T(128)S(1)}, f32[4]{0:T(128)}, u32[]{:S(2)}) copy-start(f32[4]{0:T(128)} %permittivity.1) | copy-start | bytes 52
  0.7 0.7 %copy-start.8 = (f32[4]{0:T(128)S(1)}, f32[4]{0:T(128)}, u32[]{:S(2)}) copy-start(f32[4]{0:T(128)} %contrast.1) | copy-start | bytes 52
  1.3 1.0 %copy-start = (f32[3,8,16,256]{3,2,1,0:T(8,128)S(1)}, f32[3,8,16,256]{3,2,1,0:T(8,128)}, u32[]{:S(2)}) copy-start(f32[3,8,16,256]{3,2,1,0:T(8,128)} %te.1) | copy-start | bytes 1179652
  2.3 1.0 %copy-start.1 = (f32[3,8,16,256]{3,2,1,0:T(8,128)S(1)}, f32[3,8,16,256]{3,2,1,0:T(8,128)}, u32[]{:S(2)}) copy-start(f32[3,8,16,256]{3,2,1,0:T(8,128)} %th.1) | copy-start | bytes 1179652
  3.3 0.8 %copy-start.2 = (f32[3,8,16,4]{2,3,1,0:T(4,128)S(1)}, f32[3,8,16,4]{2,3,1,0:T(4,128)}, u32[]{:S(2)}) copy-start(f32[3,8,16,4]{2,3,1,0:T(4,128)} %param.11) | copy-start | bytes 18436
  4.1 0.8 %copy-start.3 = (f32[3,8,16,4]{2,3,1,0:T(4,128)S(1)}, f32[3,8,16,4]{2,3,1,0:T(4,128)}, u32[]{:S(2)}) copy-start(f32[3,8,16,4]{2,3,1,0:T(4,128)} %param.12) | copy-start | bytes 18436
  4.9 0.7 %copy-start.4 = (s32[8,16,4]{1,2,0:T(4,128)S(1)}, s32[8,16,4]{1,2,0:T(4,128)}, u32[]{:S(2)}) copy-start(s32[8,16,4]{1,2,0:T(4,128)} %param.13) | copy-start | bytes 6148
  5.6 0.7 %copy-start.5 = (s32[8,16,4]{1,2,0:T(4,128)S(1)}, s32[8,16,4]{1,2,0:T(4,128)}, u32[]{:S(2)}) copy-start(s32[8,16,4]{1,2,0:T(4,128)} %param.14) | copy-start | bytes 6148

commit v2 on v1

--- a/solution.py
+++ b/solution.py
@@ -13,7 +13,6 @@
 LAYERS = 4
 WIDE = LAYERS * DIRS
 HALF = WIDE // 2
-HIGHEST = lax.Precision.HIGHEST
 time_step = 0.5
 
 
@@ -61,14 +60,6 @@
     low = jnp.where(near, v, pltpu.roll(v, DIRS // 2, axis))
     high = jnp.where(near, pltpu.roll(v, HALF - DIRS // 2, axis), v)
     return jnp.concatenate([low, high], axis)
-
-
-def put(buf, at, tangent, forward):
-    n = len(tangent)
-    for k in range(n):
-        buf[at, 2 * k] = tangent[k][:, :HALF]
-        buf[at, 2 * k + 1] = tangent[k][:, HALF:]
-        buf[at, 2 * n + k] = packed(forward[k])
 
 
 def take(buf, at, n):
@@ -112,37 +103,58 @@
     )
 
 
-def widened(ref, lead):
-    ny = ref.shape[-1]
+def split(v):
+    parts = []
+    for _ in range(3):
+        parts.append(v.astype(jnp.bfloat16))
+        v = v - parts[-1].astype(jnp.float32)
+    return parts
+
+
+def widened(layers, ny):
+    lead = layers[0].shape[0]
     flat = LAYERS * ny
     total = 0.0
     for z in range(LAYERS):
-        part = ref[..., z, :].reshape(lead, ny).astype(jnp.float32)
-        place = (
-            lax.broadcasted_iota(jnp.int32, (ny, flat), 1)
-            == lax.broadcasted_iota(jnp.int32, (ny, flat), 0) + z * ny
-        ).astype(jnp.float32)
-        total = total + jnp.dot(part, place, precision=HIGHEST, preferred_element_type=jnp.float32)
-    rows = jnp.broadcast_to(total[:, None, :], (lead, ny, flat))
+        for k, part in enumerate(split(layers[z])):
+            place = (
+                lax.broadcasted_iota(jnp.int32, (ny, 3 * flat), 1)
+                == lax.broadcasted_iota(jnp.int32, (ny, 3 * flat), 0) + (k * flat + z * ny)
+            ).astype(jnp.float32)
+            total = total + jnp.dot(part, place.astype(jnp.bfloat16), preferred_element_type=jnp.float32)
+    rows = jnp.broadcast_to(total[:, None, :], (lead, ny, 3 * flat))
     rows = jnp.where(lanes_of(rows.shape) % ny == sublanes_of(rows.shape), rows, 0.0)
     spread = (
-        lax.broadcasted_iota(jnp.int32, (flat, WIDE), 0) // ny
-        == lax.broadcasted_iota(jnp.int32, (flat, WIDE), 1) // DIRS
+        (lax.broadcasted_iota(jnp.int32, (3 * flat, WIDE), 0) // ny) % LAYERS
+        == lax.broadcasted_iota(jnp.int32, (3 * flat, WIDE), 1) // DIRS
     ).astype(jnp.float32)
     wide = jnp.dot(
-        rows.reshape(lead * ny, flat), spread, precision=HIGHEST, preferred_element_type=jnp.float32
+        rows.reshape(lead * ny, 3 * flat).astype(jnp.bfloat16),
+        spread.astype(jnp.bfloat16),
+        preferred_element_type=jnp.float32,
     )
     return wide.reshape(lead, ny, WIDE)
 
 
 def kernel(
     nx, ny, own,
-    te, th, fe, fh, classes, material, permittivity, contrast, orders,
+    te_at, th_at, fe_at, fh_at, classes_at, material_at, permittivity_at, contrast_at, orders_at,
     out_e, out_h, out_s,
     s_xm, r_xm, s_xp, r_xp, s_ym, r_ym, s_yp, r_yp, s_cx, r_cx, s_cy, r_cy,
     gathered, partial, arrived, table_c, table_s,
     rim_send, rim_recv, g_send, g_recv, p_send, p_recv,
+    te, th, fe, fh, classes, material, permittivity, contrast, orders, load,
 ):
+    loads = [
+        pltpu.make_async_copy(src, dst, load.at[k])
+        for k, (src, dst) in enumerate((
+            (te_at, te), (th_at, th), (fe_at, fe), (fh_at, fh), (classes_at, classes),
+            (material_at, material), (permittivity_at, permittivity), (contrast_at, contrast),
+            (orders_at, orders),
+        ))
+    ]
+    for c in loads:
+        c.start()
     wx, wy = te.shape[1], te.shape[2]
     i, j = lax.axis_index("gx"), lax.axis_index("gy")
     up, down = lax.rem(i + 1, nx), lax.rem(i + nx - 1, nx)
@@ -160,38 +172,66 @@
             device_id=device, device_id_type=pl.DeviceIdType.MESH,
         )
 
-    def exchange(step, e, h, fe, fh):
-        put(s_xm, step, [f[wx - 1] for f in (e[0], e[1], e[2], h[1], h[2])],
-            [f[wx - 1] for f in (fe[0], fe[1], fe[2], fh[1], fh[2])])
-        put(s_xp, step, [e[1][0], e[2][0]], [fe[1][0], fe[2][0]])
-        put(s_ym, step, [f[:, wy - 1, :] for f in (e[0], e[1], e[2], h[0], h[2])],
-            [f[:, wy - 1, :] for f in (fe[0], fe[1], fe[2], fh[0], fh[2])])
-        put(s_yp, step, [e[0][:, 0, :], e[2][:, 0, :]], [fe[0][:, 0, :], fe[2][:, 0, :]])
-        put(s_cx, step, [e[0][wx - 1, 0:1, :]], [fe[0][wx - 1, 0:1, :]])
-        put(s_cy, step, [e[1][0, wy - 1:wy, :]], [fe[1][0, wy - 1:wy, :]])
-        plan = (
-            (s_xm, r_xm, (up, j)), (s_ym, r_ym, (i, right)), (s_xp, r_xp, (down, j)),
-            (s_yp, r_yp, (i, left)), (s_cx, r_cx, (up, left)), (s_cy, r_cy, (down, right)),
+    def planes_of(e, h):
+        return (
+            [f[wx - 1] for f in (e[0], e[1], e[2], h[1], h[2])],
+            [f[:, wy - 1, :] for f in (e[0], e[1], e[2], h[0], h[2])],
+            [e[1][0], e[2][0]],
+            [e[0][:, 0, :], e[2][:, 0, :]],
+            [e[0][wx - 1, 0:1, :]],
+            [e[1][0, wy - 1:wy, :]],
         )
-        if step == 0:
-            pl.semaphore_wait(barrier, len(peers))
-        copies = [
-            copy(s.at[step], r.at[step], rim_send.at[step, k], rim_recv.at[step, k], device)
-            for k, (s, r, device) in enumerate(plan)
-        ]
+
+    rims = (
+        (s_xm, r_xm, (up, j)), (s_ym, r_ym, (i, right)), (s_xp, r_xp, (down, j)),
+        (s_yp, r_yp, (i, left)), (s_cx, r_cx, (up, left)), (s_cy, r_cy, (down, right)),
+    )
+
+    def put_tangent(step, e, h):
+        for (buf, _, _), planes in zip(rims, planes_of(e, h)):
+            for k, plane in enumerate(planes):
+                buf[step, 2 * k] = plane[:, :HALF]
+                buf[step, 2 * k + 1] = plane[:, HALF:]
+
+    def put_forward(step, e, h):
+        for (buf, _, _), planes in zip(rims, planes_of(e, h)):
+            for k, plane in enumerate(planes):
+                buf[step, 2 * len(planes) + k] = packed(plane)
+
+    def send(step, first, part):
+        copies = []
+        for k, (s, r, device) in enumerate(rims):
+            n = s.shape[1] // 3
+            span = (pl.ds(0, 3 * n), pl.ds(0, 2 * n), pl.ds(2 * n, n))[part]
+            copies.append(copy(
+                s.at[step, span], r.at[step, span], rim_send.at[first + k], rim_recv.at[first + k], device
+            ))
         for c in copies:
             c.start()
         return copies
 
+    for c in loads[:2]:
+        c.wait()
     e = [te[c] for c in range(3)]
     h = [th[c] for c in range(3)]
-    wide_e = widened(fe, 3 * wx)
-    wide_h = widened(fh, 3 * wx)
-    fwd_e = [wide_e[c * wx:(c + 1) * wx] for c in range(3)]
-    fwd_h = [wide_h[c * wx:(c + 1) * wx] for c in range(3)]
-    waiting = exchange(0, e, h, fwd_e, fwd_h)
-
-    kind = widened(material, wx)
+    put_tangent(0, e, h)
+    pl.semaphore_wait(barrier, len(peers))
+    waiting = send(0, 0, 1)
+    for c in loads[2:]:
+        c.wait()
+    layers = []
+    for z in range(LAYERS):
+        layers.append(jnp.concatenate([
+            fe[:, :, z, :].reshape(3 * wx, wy), fh[:, :, z, :].reshape(3 * wx, wy),
+            classes[:, z, :].astype(jnp.float32), material[:, z, :].astype(jnp.float32),
+        ], 0))
+    wide = widened(layers, wy)
+    fwd_e = [wide[c * wx:(c + 1) * wx] for c in range(3)]
+    fwd_h = [wide[c * wx:(c + 1) * wx] for c in range(3, 6)]
+    put_forward(0, fwd_e, fwd_h)
+    waiting += send(0, 6, 2)
+
+    kind = wide[7 * wx:]
     eps = jnp.zeros_like(kind)
     slope = jnp.zeros_like(kind)
     for k in range(permittivity.shape[0]):
@@ -199,7 +239,7 @@
         slope = jnp.where(kind == float(k), contrast[k], slope)
     inverse = time_step / eps
     coef = time_step * slope / (eps * eps)
-    hot = widened(classes, wx) == (lanes_of(kind.shape) % DIRS).astype(jnp.float32)
+    hot = wide[6 * wx:7 * wx] == (lanes_of(kind.shape) % DIRS).astype(jnp.float32)
     coef = jnp.where(hot, coef, 0.0)
 
     rows, cells = nx * own, ny * wx * wy
@@ -218,8 +258,13 @@
     index = pair[:, 0:1] * x_at + pair[:, 1:2] * y_at
     index = index - float(all_x * all_y) * jnp.round(index * (1.0 / (all_x * all_y)))
     turn = index * (1.0 / (all_x * all_y))
-    table_c[...] = sine(0.25 - jnp.abs(turn))
-    table_s[...] = sine(jnp.where(turn > 0.25, 0.5 - turn, jnp.where(turn < -0.25, -0.5 - turn, turn)))
+    cosine = sine(0.25 - jnp.abs(turn))
+    sines = sine(jnp.where(turn > 0.25, 0.5 - turn, jnp.where(turn < -0.25, -0.5 - turn, turn)))
+    for table, value in ((table_c, cosine), (table_s, sines)):
+        near, far = split(value)[:2]
+        table[:, :cells] = near
+        table[:, cells:2 * cells] = far
+        table[:, 2 * cells:] = near
 
     for step in range(STEPS):
         for c in waiting:
@@ -234,7 +279,9 @@
         tan_c = curl_b(h, rim)
         e = [e[c] + inverse * tan_c[c] - coef * fwd_c[c] for c in range(3)]
         if step < STEPS - 1:
-            waiting = exchange(step + 1, e, h, fwd_e, fwd_h)
+            put_tangent(step + 1, e, h)
+            put_forward(step + 1, fwd_e, fwd_h)
+            waiting = send(step + 1, 12 + 6 * step, 0)
 
     top_x, top_y = e[0][:, :, HALF:], e[1][:, :, HALF:]
     top = jnp.where(lanes_of(top_x.shape) < DIRS, pltpu.roll(top_x, DIRS, 2), top_y)
@@ -251,8 +298,10 @@
     for c in copies:
         c.wait()
     every = gathered[...].reshape(cells, 2 * DIRS)
-    real = jnp.dot(table_c[...], every, precision=HIGHEST, preferred_element_type=jnp.float32)
-    imag = jnp.dot(table_s[...], every, precision=HIGHEST, preferred_element_type=jnp.float32)
+    near, far = split(every)[:2]
+    every = jnp.concatenate([near, near, far], 0)
+    real = jnp.dot(table_c[...], every, preferred_element_type=jnp.float32)
+    imag = jnp.dot(table_s[...], every, preferred_element_type=jnp.float32)
     for k in range(nx):
         partial[k, 0] = real[k * own:(k + 1) * own]
         partial[k, 1] = imag[k * own:(k + 1) * own]
@@ -280,7 +329,11 @@
     rows, cells = nx * own, ny * wx * wy
     f32 = jnp.float32
     vmem = pl.BlockSpec(memory_space=pltpu.VMEM)
-    smem = pl.BlockSpec(memory_space=pltpu.SMEM)
+    args = (
+        te, th, jnp.transpose(fe, (0, 1, 3, 2)), jnp.transpose(fh, (0, 1, 3, 2)),
+        jnp.transpose(classes, (0, 2, 1)), jnp.transpose(material, (0, 2, 1)),
+        permittivity, contrast, jnp.transpose(orders),
+    )
 
     def two(*shape):
         return [pltpu.VMEM((STEPS,) + shape, f32)] * 2
@@ -292,7 +345,7 @@
             jax.ShapeDtypeStruct(th.shape, f32),
             jax.ShapeDtypeStruct((own, 4 * DIRS), f32),
         ),
-        in_specs=[vmem] * 6 + [smem] * 2 + [vmem],
+        in_specs=[pl.BlockSpec(memory_space=pltpu.HBM)] * 9,
         out_specs=(vmem, vmem, vmem),
         scratch_shapes=[
             *two(15, wy, HALF), *two(6, wy, HALF), *two(15, wx, HALF), *two(6, wx, HALF),
@@ -300,21 +353,21 @@
             pltpu.VMEM((ny, wx * wy, 2 * DIRS), f32),
             pltpu.VMEM((nx, 2, own, 2 * DIRS), f32),
             pltpu.VMEM((nx - 1, 2, own, 2 * DIRS), f32),
-            pltpu.VMEM((rows, cells), f32),
-            pltpu.VMEM((rows, cells), f32),
-            pltpu.SemaphoreType.DMA((STEPS, 6)), pltpu.SemaphoreType.DMA((STEPS, 6)),
+            pltpu.VMEM((rows, 3 * cells), jnp.bfloat16),
+            pltpu.VMEM((rows, 3 * cells), jnp.bfloat16),
+            pltpu.SemaphoreType.DMA((6 * STEPS + 6,)), pltpu.SemaphoreType.DMA((6 * STEPS + 6,)),
             pltpu.SemaphoreType.DMA((ny,)), pltpu.SemaphoreType.DMA((ny,)),
             pltpu.SemaphoreType.DMA((nx,)), pltpu.SemaphoreType.DMA((nx,)),
+            *[pltpu.VMEM(v.shape, v.dtype) for v in args[:6]],
+            *[pltpu.SMEM(v.shape, v.dtype) for v in args[6:8]],
+            pltpu.VMEM(args[8].shape, args[8].dtype),
+            pltpu.SemaphoreType.DMA((9,)),
         ],
         compiler_params=pltpu.CompilerParams(
-            collective_id=0, has_side_effects=True, vmem_limit_bytes=40 * 1024 * 1024
+            collective_id=0, has_side_effects=True, vmem_limit_bytes=64 * 1024 * 1024 - 65536
         ),
         name="slab",
-    )(
-        te, th, jnp.transpose(fe, (0, 1, 3, 2)), jnp.transpose(fh, (0, 1, 3, 2)),
-        jnp.transpose(classes, (0, 2, 1)), jnp.transpose(material, (0, 2, 1)),
-        permittivity, contrast, jnp.transpose(orders),
-    )
+    )(*args)
 
 
 def solution(mesh):

time: 37 us -> 32.2 us (0.87)
  local copies, waits for them, and re-layouts: 7.81 us -> 3.19 us
    unnamed x21 -> x7, local copies, waits for them, and re-layouts: 7.81 us -> 3.19 us
where the time goes in v2:
time: 32.2 us; the launch traced here: 31.9 us
  Pallas kernels  28.1 us (87%)
  local copies, waits for them, and re-layouts  3.19 us (10%)
  between operations  0.65 us (2%)
    pallas_call x1, Pallas kernels, local(): pl.pallas_call(functools.partial(kernel, nx, ny, own), out_shape=(jax.Sha...  28.1 us
    unnamed x7, local copies, waits for them, and re-layouts  3.19 us

profile of v2, /device:TPU:1, one launch (start us, length us, event | category | flops | bytes accessed | tf_op | source)
XLA Modules:
  0.0 31.9 jit_solution(3434000704793435019)
XLA Ops:
  0.6 28.1 %slab.1 = (f32[3,8,16,256]{3,2,1,0:T(8,128)}, f32[3,8,16,256]{3,2,1,0:T(8,128)}, f32[32,256]{1,0:T(8,128)}) custom-call(f32[3,8,16,256]{3,2,1,0:T(8,128)} %te_at.1, f32[3,8,16,256]{3,2,1,0:T(8,128)} %th_at.1, f32[3,8,4,16]{3,2,1,0:T(4,128)} %bitcast.5, f32[3,8,4,16]{3,2,1,0:T(4,128)} %bitcast.6, s32[8,4,16]{2,1,0:T(4,128)} %bitcast.7, s32[8,4,16]{2,1,0:T(4,128)} %bitcast.8, ...), custom_call_target="tpu_custom_call" | custom-call | tf_op jit(solution)/shard_map/slab/pallas_call | solution.py:341
  28.7 0.0 copy-start
  28.7 1.8 %copy.15 = f32[3,8,16,256]{3,2,1,0:T(8,128)} copy(f32[3,8,16,256]{3,2,1,0:T(8,128)} %get-tuple-element.6) | data formatting | bytes 786432
  30.6 0.0 copy-done
  30.6 0.0 copy-start.1
  30.6 0.7 %copy.16 = f32[3,8,16,256]{3,2,1,0:T(8,128)} copy(f32[3,8,16,256]{3,2,1,0:T(8,128)S(1)} %copy-done) | data formatting | bytes 786432
  31.3 0.0 copy-done.1
  31.3 0.6 %copy.17 = f32[32,256]{1,0:T(8,128)} copy(f32[32,256]{1,0:T(8,128)S(1)} %copy-done.1) | data formatting | bytes 65536
Async XLA Ops:
  28.7 1.8 %copy-start = (f32[3,8,16,256]{3,2,1,0:T(8,128)S(1)}, f32[3,8,16,256]{3,2,1,0:T(8,128)}, u32[]{:S(2)}) copy-start(f32[3,8,16,256]{3,2,1,0:T(8,128)} %get-tuple-element.7) | copy-start | bytes 1179652
  30.6 0.8 %copy-start.1 = (f32[32,256]{1,0:T(8,128)S(1)}, f32[32,256]{1,0:T(8,128)}, u32[]{:S(2)}) copy-start(f32[32,256]{1,0:T(8,128)} %get-tuple-element.8) | copy-start | bytes 98308

commit v3 on v2

--- a/solution.py
+++ b/solution.py
@@ -141,9 +141,9 @@
     te_at, th_at, fe_at, fh_at, classes_at, material_at, permittivity_at, contrast_at, orders_at,
     out_e, out_h, out_s,
     s_xm, r_xm, s_xp, r_xp, s_ym, r_ym, s_yp, r_yp, s_cx, r_cx, s_cy, r_cy,
-    gathered, partial, arrived, table_c, table_s,
+    gathered, partial, paired, summed, arrived, table_c, table_s,
     rim_send, rim_recv, g_send, g_recv, p_send, p_recv,
-    te, th, fe, fh, classes, material, permittivity, contrast, orders, load,
+    te, th, fe, fh, classes, material, permittivity, contrast, orders, load, new_e, new_h, store,
 ):
     loads = [
         pltpu.make_async_copy(src, dst, load.at[k])
@@ -160,7 +160,8 @@
     up, down = lax.rem(i + 1, nx), lax.rem(i + nx - 1, nx)
     right, left = lax.rem(j + 1, ny), lax.rem(j + ny - 1, ny)
     barrier = pltpu.get_barrier_semaphore()
-    peers = [(lax.rem(i + d, nx), j) for d in range(1, nx)]
+    offsets = sorted({1, nx - 1, *range(2, nx, 2)})
+    peers = [(lax.rem(i + d, nx), j) for d in offsets]
     peers += [(i, lax.rem(j + d, ny)) for d in range(1, ny)]
     peers += [(up, left), (down, right)]
     for peer in peers:
@@ -293,8 +294,14 @@
     for c in copies:
         c.start()
     for c in range(3):
-        out_e[c] = e[c]
-        out_h[c] = h[c]
+        new_e[c] = e[c]
+        new_h[c] = h[c]
+    stores = [
+        pltpu.make_async_copy(new_e, out_e, store.at[0]),
+        pltpu.make_async_copy(new_h, out_h, store.at[1]),
+    ]
+    for c in stores:
+        c.start()
     for c in copies:
         c.wait()
     every = gathered[...].reshape(cells, 2 * DIRS)
@@ -305,22 +312,53 @@
     for k in range(nx):
         partial[k, 0] = real[k * own:(k + 1) * own]
         partial[k, 1] = imag[k * own:(k + 1) * own]
+    core = lax.rem(i, 2)
+    mate = i + 1 - 2 * core
+    chips = nx // 2
+    order = list(range(1, chips)) + [0]
+    pairs = {
+        d: copy(
+            partial.at[lax.rem(mate + 2 * d, nx)], paired.at[d], p_send.at[d], p_recv.at[d], (mate, j)
+        )
+        for d in order
+    }
+    for d in order:
+        pairs[d].start()
     copies = []
-    for d in range(1, nx):
-        peer = lax.rem(i + d, nx)
-        copies.append(copy(partial.at[peer], arrived.at[d - 1], p_send.at[d], p_recv.at[d], (peer, j)))
-    for c in copies:
-        c.start()
-    total = partial[i]
-    for c in copies:
-        c.wait()
-    for d in range(nx - 1):
+    for d in order:
+        mine = lax.rem(i + 2 * d, nx)
+        pairs[d].wait_recv()
+        if d:
+            summed[d] = partial[mine] + paired[d]
+            c = copy(summed.at[d], arrived.at[d], p_send.at[chips + d], p_recv.at[chips + d], (mine, j))
+            c.start()
+            copies.append(c)
+    total = partial[i] + paired[0]
+    for d, c in zip(order, copies):
+        c.wait_recv()
         total = total + arrived[d]
+    for c in copies + [pairs[d] for d in order]:
+        c.wait_send()
     scale = 1.0 / math.sqrt(all_x * all_y)
     re, im = total[0] * scale, total[1] * -scale
     low = lanes_of(re.shape) < DIRS
     out_s[:, :2 * DIRS] = jnp.where(low, re, pltpu.roll(im, DIRS, 1))
     out_s[:, 2 * DIRS:] = jnp.where(low, pltpu.roll(re, DIRS, 1), im)
+    for c in stores:
+        c.wait()
+
+
+def hand_over(from_e, from_h, from_s, to_e, to_h, to_s, via_e, via_h, via_s, sem):
+    plan = ((from_e, via_e, to_e), (from_h, via_h, to_h), (from_s, via_s, to_s))
+    loads = [pltpu.make_async_copy(src, via, sem.at[0, k]) for k, (src, via, _) in enumerate(plan)]
+    stores = [pltpu.make_async_copy(via, dst, sem.at[1, k]) for k, (_, via, dst) in enumerate(plan)]
+    for c in loads:
+        c.start()
+    for load, store in zip(loads, stores):
+        load.wait()
+        store.start()
+    for c in stores:
+        c.wait()
 
 
 def local(nx, ny, te, th, fe, fh, classes, material, permittivity, contrast, orders):
@@ -338,21 +376,23 @@
     def two(*shape):
         return [pltpu.VMEM((STEPS,) + shape, f32)] * 2
 
-    return pl.pallas_call(
+    hbm = pl.BlockSpec(memory_space=pltpu.HBM)
+    out_shape = (
+        jax.ShapeDtypeStruct(te.shape, f32),
+        jax.ShapeDtypeStruct(th.shape, f32),
+        jax.ShapeDtypeStruct((own, 4 * DIRS), f32),
+    )
+    results = pl.pallas_call(
         functools.partial(kernel, nx, ny, own),
-        out_shape=(
-            jax.ShapeDtypeStruct(te.shape, f32),
-            jax.ShapeDtypeStruct(th.shape, f32),
-            jax.ShapeDtypeStruct((own, 4 * DIRS), f32),
-        ),
-        in_specs=[pl.BlockSpec(memory_space=pltpu.HBM)] * 9,
-        out_specs=(vmem, vmem, vmem),
+        out_shape=out_shape,
+        in_specs=[hbm] * 9,
+        out_specs=(hbm, hbm, vmem),
         scratch_shapes=[
             *two(15, wy, HALF), *two(6, wy, HALF), *two(15, wx, HALF), *two(6, wx, HALF),
             *two(3, 1, HALF), *two(3, 1, HALF),
             pltpu.VMEM((ny, wx * wy, 2 * DIRS), f32),
             pltpu.VMEM((nx, 2, own, 2 * DIRS), f32),
-            pltpu.VMEM((nx - 1, 2, own, 2 * DIRS), f32),
+            *[pltpu.VMEM((nx // 2, 2, own, 2 * DIRS), f32)] * 3,
             pltpu.VMEM((rows, 3 * cells), jnp.bfloat16),
             pltpu.VMEM((rows, 3 * cells), jnp.bfloat16),
             pltpu.SemaphoreType.DMA((6 * STEPS + 6,)), pltpu.SemaphoreType.DMA((6 * STEPS + 6,)),
@@ -362,12 +402,23 @@
             *[pltpu.SMEM(v.shape, v.dtype) for v in args[6:8]],
             pltpu.VMEM(args[8].shape, args[8].dtype),
             pltpu.SemaphoreType.DMA((9,)),
+            pltpu.VMEM(te.shape, f32), pltpu.VMEM(th.shape, f32),
+            pltpu.SemaphoreType.DMA((2,)),
         ],
         compiler_params=pltpu.CompilerParams(
             collective_id=0, has_side_effects=True, vmem_limit_bytes=64 * 1024 * 1024 - 65536
         ),
         name="slab",
     )(*args)
+    return pl.pallas_call(
+        hand_over,
+        out_shape=out_shape,
+        in_specs=[hbm] * 3,
+        out_specs=(hbm, hbm, hbm),
+        scratch_shapes=[pltpu.VMEM(v.shape, f32) for v in out_shape] + [pltpu.SemaphoreType.DMA((2, 3))],
+        compiler_params=pltpu.CompilerParams(vmem_limit_bytes=64 * 1024 * 1024 - 65536),
+        name="hand_over",
+    )(*results)
 
 
 def solution(mesh):

time: 32.2 us -> 30.7 us (0.953)
  the two profiles are of different devices: /device:TPU:1 before, /device:TPU:0 now
where the time goes in v3:
time: 30.7 us; the launch traced here: 30.6 us
  Pallas kernels  29.9 us (97%)
  between operations  0.64 us (2%)
    pallas_call x1, Pallas kernels, local(): pl.pallas_call(functools.partial(kernel, nx, ny, own), out_shape=out_shap...  28 us
    pallas_call x1, Pallas kernels, local(): pl.pallas_call(hand_over, out_shape=out_shape, in_specs=[hbm] * 3, out_sp...  1.93 us

profile of v3, /device:TPU:0, one launch (start us, length us, event | category | flops | bytes accessed | tf_op | source)
XLA Modules:
  0.0 30.6 jit_solution(2489694119447309263)
XLA Ops:
  0.6 28.0 %slab.1 = (f32[3,8,16,256]{3,2,1,0:T(8,128)}, f32[3,8,16,256]{3,2,1,0:T(8,128)}, f32[32,256]{1,0:T(8,128)}) custom-call(f32[3,8,16,256]{3,2,1,0:T(8,128)} %te_at.1, f32[3,8,16,256]{3,2,1,0:T(8,128)} %th_at.1, f32[3,8,4,16]{3,2,1,0:T(4,128)} %bitcast.5, f32[3,8,4,16]{3,2,1,0:T(4,128)} %bitcast.6, s32[8,4,16]{2,1,0:T(4,128)} %bitcast.7, s32[8,4,16]{2,1,0:T(4,128)} %bitcast.8, ...), custom_call_target="tpu_custom_call" | custom-call | tf_op jit(solution)/shard_map/slab/pallas_call | solution.py:385
  28.7 1.9 %hand_over.1 = (f32[3,8,16,256]{3,2,1,0:T(8,128)}, f32[3,8,16,256]{3,2,1,0:T(8,128)}, f32[32,256]{1,0:T(8,128)}) custom-call(f32[3,8,16,256]{3,2,1,0:T(8,128)} %get-tuple-element.6.from_e, f32[3,8,16,256]{3,2,1,0:T(8,128)} %get-tuple-element.7.from_h, f32[32,256]{1,0:T(8,128)} %get-tuple-element.8.from_s), custom_call_target="tpu_custom_call" | custom-call | tf_op jit(solution)/shard_map/hand_over/pallas_call | solution.py:413

commit v4 on v3

--- a/solution.py
+++ b/solution.py
@@ -141,14 +141,15 @@
     te_at, th_at, fe_at, fh_at, classes_at, material_at, permittivity_at, contrast_at, orders_at,
     out_e, out_h, out_s,
     s_xm, r_xm, s_xp, r_xp, s_ym, r_ym, s_yp, r_yp, s_cx, r_cx, s_cy, r_cy,
-    gathered, partial, paired, summed, arrived, table_c, table_s,
+    gathered, partial, paired, summed, arrived, table,
     rim_send, rim_recv, g_send, g_recv, p_send, p_recv,
     te, th, fe, fh, classes, material, permittivity, contrast, orders, load, new_e, new_h, store,
 ):
     loads = [
         pltpu.make_async_copy(src, dst, load.at[k])
         for k, (src, dst) in enumerate((
-            (te_at, te), (th_at, th), (fe_at, fe), (fh_at, fh), (classes_at, classes),
+            *[(src.at[c], dst.at[c]) for c in range(3) for src, dst in ((te_at, te), (th_at, th))],
+            (fe_at, fe), (fh_at, fh), (classes_at, classes),
             (material_at, material), (permittivity_at, permittivity), (contrast_at, contrast),
             (orders_at, orders),
         ))
@@ -175,17 +176,17 @@
 
     def planes_of(e, h):
         return (
+            [f[:, wy - 1, :] for f in (e[0], e[1], e[2], h[0], h[2])],
             [f[wx - 1] for f in (e[0], e[1], e[2], h[1], h[2])],
-            [f[:, wy - 1, :] for f in (e[0], e[1], e[2], h[0], h[2])],
+            [e[0][:, 0, :], e[2][:, 0, :]],
             [e[1][0], e[2][0]],
-            [e[0][:, 0, :], e[2][:, 0, :]],
             [e[0][wx - 1, 0:1, :]],
             [e[1][0, wy - 1:wy, :]],
         )
 
     rims = (
-        (s_xm, r_xm, (up, j)), (s_ym, r_ym, (i, right)), (s_xp, r_xp, (down, j)),
-        (s_yp, r_yp, (i, left)), (s_cx, r_cx, (up, left)), (s_cy, r_cy, (down, right)),
+        (s_ym, r_ym, (i, right)), (s_xm, r_xm, (up, j)), (s_yp, r_yp, (i, left)),
+        (s_xp, r_xp, (down, j)), (s_cx, r_cx, (up, left)), (s_cy, r_cy, (down, right)),
     )
 
     def put_tangent(step, e, h):
@@ -211,14 +212,14 @@
             c.start()
         return copies
 
-    for c in loads[:2]:
+    for c in loads[:6]:
         c.wait()
     e = [te[c] for c in range(3)]
     h = [th[c] for c in range(3)]
     put_tangent(0, e, h)
     pl.semaphore_wait(barrier, len(peers))
     waiting = send(0, 0, 1)
-    for c in loads[2:]:
+    for c in loads[6:]:
         c.wait()
     layers = []
     for z in range(LAYERS):
@@ -261,11 +262,12 @@
     turn = index * (1.0 / (all_x * all_y))
     cosine = sine(0.25 - jnp.abs(turn))
     sines = sine(jnp.where(turn > 0.25, 0.5 - turn, jnp.where(turn < -0.25, -0.5 - turn, turn)))
-    for table, value in ((table_c, cosine), (table_s, sines)):
+    block = wx * wy
+    for at, value in ((0, cosine), (rows, sines)):
         near, far = split(value)[:2]
-        table[:, :cells] = near
-        table[:, cells:2 * cells] = far
-        table[:, 2 * cells:] = near
+        for k in range(ny):
+            for q, part in enumerate((near, far, near)):
+                table[k, at:at + rows, q * block:(q + 1) * block] = part[:, k * block:(k + 1) * block]
 
     for step in range(STEPS):
         for c in waiting:
@@ -302,16 +304,21 @@
     ]
     for c in stores:
         c.start()
+    def product(source):
+        near, far = split(gathered[source])[:2]
+        return jnp.dot(
+            table[source], jnp.concatenate([near, near, far], 0), preferred_element_type=jnp.float32
+        )
+
+    sums = product(j)
+    for d, c in zip(range(1, ny), copies):
+        c.wait_recv()
+        sums = sums + product(lax.rem(j + ny - d, ny))
     for c in copies:
-        c.wait()
-    every = gathered[...].reshape(cells, 2 * DIRS)
-    near, far = split(every)[:2]
-    every = jnp.concatenate([near, near, far], 0)
-    real = jnp.dot(table_c[...], every, preferred_element_type=jnp.float32)
-    imag = jnp.dot(table_s[...], every, preferred_element_type=jnp.float32)
+        c.wait_send()
     for k in range(nx):
-        partial[k, 0] = real[k * own:(k + 1) * own]
-        partial[k, 1] = imag[k * own:(k + 1) * own]
+        partial[k, 0] = sums[k * own:(k + 1) * own]
+        partial[k, 1] = sums[rows + k * own:rows + (k + 1) * own]
     core = lax.rem(i, 2)
     mate = i + 1 - 2 * core
     chips = nx // 2
@@ -349,7 +356,11 @@
 
 
 def hand_over(from_e, from_h, from_s, to_e, to_h, to_s, via_e, via_h, via_s, sem):
-    plan = ((from_e, via_e, to_e), (from_h, via_h, to_h), (from_s, via_s, to_s))
+    plan = [
+        (src.at[c], via.at[c], dst.at[c])
+        for c in range(3) for src, via, dst in ((from_e, via_e, to_e), (from_h, via_h, to_h))
+    ]
+    plan.append((from_s, via_s, to_s))
     loads = [pltpu.make_async_copy(src, via, sem.at[0, k]) for k, (src, via, _) in enumerate(plan)]
     stores = [pltpu.make_async_copy(via, dst, sem.at[1, k]) for k, (_, via, dst) in enumerate(plan)]
     for c in loads:
@@ -364,7 +375,7 @@
 def local(nx, ny, te, th, fe, fh, classes, material, permittivity, contrast, orders):
     wx, wy = te.shape[1], te.shape[2]
     own = orders.shape[0] // (nx * ny)
-    rows, cells = nx * own, ny * wx * wy
+    rows = nx * own
     f32 = jnp.float32
     vmem = pl.BlockSpec(memory_space=pltpu.VMEM)
     args = (
@@ -393,15 +404,14 @@
             pltpu.VMEM((ny, wx * wy, 2 * DIRS), f32),
             pltpu.VMEM((nx, 2, own, 2 * DIRS), f32),
             *[pltpu.VMEM((nx // 2, 2, own, 2 * DIRS), f32)] * 3,
-            pltpu.VMEM((rows, 3 * cells), jnp.bfloat16),
-            pltpu.VMEM((rows, 3 * cells), jnp.bfloat16),
+            pltpu.VMEM((ny, 2 * rows, 3 * wx * wy), jnp.bfloat16),
             pltpu.SemaphoreType.DMA((6 * STEPS + 6,)), pltpu.SemaphoreType.DMA((6 * STEPS + 6,)),
             pltpu.SemaphoreType.DMA((ny,)), pltpu.SemaphoreType.DMA((ny,)),
             pltpu.SemaphoreType.DMA((nx,)), pltpu.SemaphoreType.DMA((nx,)),
             *[pltpu.VMEM(v.shape, v.dtype) for v in args[:6]],
             *[pltpu.SMEM(v.shape, v.dtype) for v in args[6:8]],
             pltpu.VMEM(args[8].shape, args[8].dtype),
-            pltpu.SemaphoreType.DMA((9,)),
+            pltpu.SemaphoreType.DMA((13,)),
             pltpu.VMEM(te.shape, f32), pltpu.VMEM(th.shape, f32),
             pltpu.SemaphoreType.DMA((2,)),
         ],
@@ -415,7 +425,7 @@
         out_shape=out_shape,
         in_specs=[hbm] * 3,
         out_specs=(hbm, hbm, hbm),
-        scratch_shapes=[pltpu.VMEM(v.shape, f32) for v in out_shape] + [pltpu.SemaphoreType.DMA((2, 3))],
+        scratch_shapes=[pltpu.VMEM(v.shape, f32) for v in out_shape] + [pltpu.SemaphoreType.DMA((2, 7))],
         compiler_params=pltpu.CompilerParams(vmem_limit_bytes=64 * 1024 * 1024 - 65536),
         name="hand_over",
     )(*results)

time: 30.7 us -> 30.7 us (level)
  no operation moved by 1% of the time
where the time goes in v4:
time: 30.7 us; the launch traced here: 30.6 us
  Pallas kernels  29.9 us (97%)
  between operations  0.64 us (2%)
    pallas_call x1, Pallas kernels, local(): pl.pallas_call(functools.partial(kernel, nx, ny, own), out_shape=out_shap...  27.9 us
    pallas_call x1, Pallas kernels, local(): pl.pallas_call(hand_over, out_shape=out_shape, in_specs=[hbm] * 3, out_sp...  1.99 us

profile of v4, /device:TPU:0, one launch (start us, length us, event | category | flops | bytes accessed | tf_op | source)
XLA Modules:
  0.0 30.6 jit_solution(14534314387315832647)
XLA Ops:
  0.6 27.9 %slab.1 = (f32[3,8,16,256]{3,2,1,0:T(8,128)}, f32[3,8,16,256]{3,2,1,0:T(8,128)}, f32[32,256]{1,0:T(8,128)}) custom-call(f32[3,8,16,256]{3,2,1,0:T(8,128)} %te_at.1, f32[3,8,16,256]{3,2,1,0:T(8,128)} %th_at.1, f32[3,8,4,16]{3,2,1,0:T(4,128)} %bitcast.5, f32[3,8,4,16]{3,2,1,0:T(4,128)} %bitcast.6, s32[8,4,16]{2,1,0:T(4,128)} %bitcast.7, s32[8,4,16]{2,1,0:T(4,128)} %bitcast.8, ...), custom_call_target="tpu_custom_call" | custom-call | tf_op jit(solution)/shard_map/slab/pallas_call | solution.py:396
  28.6 2.0 %hand_over.1 = (f32[3,8,16,256]{3,2,1,0:T(8,128)}, f32[3,8,16,256]{3,2,1,0:T(8,128)}, f32[32,256]{1,0:T(8,128)}) custom-call(f32[3,8,16,256]{3,2,1,0:T(8,128)} %get-tuple-element.6.from_e, f32[3,8,16,256]{3,2,1,0:T(8,128)} %get-tuple-element.7.from_h, f32[32,256]{1,0:T(8,128)} %get-tuple-element.8.from_s), custom_call_target="tpu_custom_call" | custom-call | tf_op jit(solution)/shard_map/hand_over/pallas_call | solution.py:423

commit v5 on v4

--- a/solution.py
+++ b/solution.py
@@ -62,9 +62,31 @@
     return jnp.concatenate([low, high], axis)
 
 
+SHARE = 4
+PIECE = DIRS // 2 // SHARE
+
+
+def dense(planes):
+    values = [packed(p) for p in planes]
+    place = lanes_of(values[0].shape) % (DIRS // 2) // PIECE
+    result = values[0]
+    for q in range(1, len(values)):
+        result = jnp.where(place == q, values[q], result)
+    return result
+
+
+def plane_of(v, q):
+    place = lanes_of(v.shape) % (DIRS // 2) // PIECE
+    result = v
+    for r in range(SHARE):
+        if r != q:
+            result = jnp.where(place == r, pltpu.roll(v, (PIECE * (r - q)) % HALF, v.ndim - 1), result)
+    return unpacked(result)
+
+
 def take(buf, at, n):
     tangent = [jnp.concatenate([buf[at, 2 * k], buf[at, 2 * k + 1]], -1) for k in range(n)]
-    forward = [unpacked(buf[at, 2 * n + k]) for k in range(n)]
+    forward = [plane_of(buf[at, 2 * n + k // SHARE], k % SHARE) for k in range(n)]
     return (tangent, forward)
 
 
@@ -197,14 +219,16 @@
 
     def put_forward(step, e, h):
         for (buf, _, _), planes in zip(rims, planes_of(e, h)):
-            for k, plane in enumerate(planes):
-                buf[step, 2 * len(planes) + k] = packed(plane)
+            n = len(planes)
+            for k in range(0, n, SHARE):
+                buf[step, 2 * n + k // SHARE] = dense(planes[k:k + SHARE])
 
     def send(step, first, part):
         copies = []
         for k, (s, r, device) in enumerate(rims):
-            n = s.shape[1] // 3
-            span = (pl.ds(0, 3 * n), pl.ds(0, 2 * n), pl.ds(2 * n, n))[part]
+            n = (5, 5, 2, 2, 1, 1)[k]
+            extra = s.shape[1] - 2 * n
+            span = (pl.ds(0, 2 * n + extra), pl.ds(0, 2 * n), pl.ds(2 * n, extra))[part]
             copies.append(copy(
                 s.at[step, span], r.at[step, span], rim_send.at[first + k], rim_recv.at[first + k], device
             ))
@@ -399,7 +423,7 @@
         in_specs=[hbm] * 9,
         out_specs=(hbm, hbm, vmem),
         scratch_shapes=[
-            *two(15, wy, HALF), *two(6, wy, HALF), *two(15, wx, HALF), *two(6, wx, HALF),
+            *two(12, wy, HALF), *two(5, wy, HALF), *two(12, wx, HALF), *two(5, wx, HALF),
             *two(3, 1, HALF), *two(3, 1, HALF),
             pltpu.VMEM((ny, wx * wy, 2 * DIRS), f32),
             pltpu.VMEM((nx, 2, own, 2 * DIRS), f32),

time: 30.7 us -> 30.8 us (level)
  no operation moved by 1% of the time
where the time goes in v5:
time: 30.8 us; the launch traced here: 30.7 us
  Pallas kernels  30 us (97%)
  between operations  0.64 us (2%)
    pallas_call x1, Pallas kernels, local(): pl.pallas_call(functools.partial(kernel, nx, ny, own), out_shape=out_shap...  28 us
    pallas_call x1, Pallas kernels, local(): pl.pallas_call(hand_over, out_shape=out_shape, in_specs=[hbm] * 3, out_sp...  1.99 us

profile of v5, /device:TPU:0, one launch (start us, length us, event | category | flops | bytes accessed | tf_op | source)
XLA Modules:
  0.0 30.7 jit_solution(6923936183354395601)
XLA Ops:
  0.6 28.0 %slab.1 = (f32[3,8,16,256]{3,2,1,0:T(8,128)}, f32[3,8,16,256]{3,2,1,0:T(8,128)}, f32[32,256]{1,0:T(8,128)}) custom-call(f32[3,8,16,256]{3,2,1,0:T(8,128)} %te_at.1, f32[3,8,16,256]{3,2,1,0:T(8,128)} %th_at.1, f32[3,8,4,16]{3,2,1,0:T(4,128)} %bitcast.5, f32[3,8,4,16]{3,2,1,0:T(4,128)} %bitcast.6, s32[8,4,16]{2,1,0:T(4,128)} %bitcast.7, s32[8,4,16]{2,1,0:T(4,128)} %bitcast.8, ...), custom_call_target="tpu_custom_call" | custom-call | tf_op jit(solution)/shard_map/slab/pallas_call | solution.py:420
  28.7 2.0 %hand_over.1 = (f32[3,8,16,256]{3,2,1,0:T(8,128)}, f32[3,8,16,256]{3,2,1,0:T(8,128)}, f32[32,256]{1,0:T(8,128)}) custom-call(f32[3,8,16,256]{3,2,1,0:T(8,128)} %get-tuple-element.6.from_e, f32[3,8,16,256]{3,2,1,0:T(8,128)} %get-tuple-element.7.from_h, f32[32,256]{1,0:T(8,128)} %get-tuple-element.8.from_s), custom_call_target="tpu_custom_call" | custom-call | tf_op jit(solution)/shard_map/hand_over/pallas_call | solution.py:447

commit v6 on v5

--- a/solution.py
+++ b/solution.py
@@ -176,8 +176,6 @@
             (orders_at, orders),
         ))
     ]
-    for c in loads:
-        c.start()
     wx, wy = te.shape[1], te.shape[2]
     i, j = lax.axis_index("gx"), lax.axis_index("gy")
     up, down = lax.rem(i + 1, nx), lax.rem(i + nx - 1, nx)
@@ -189,6 +187,8 @@
     peers += [(up, left), (down, right)]
     for peer in peers:
         pl.semaphore_signal(barrier, inc=1, device_id=peer, device_id_type=pl.DeviceIdType.MESH)
+    for c in loads:
+        c.start()
 
     def copy(src, dst, send, recv, device):
         return pltpu.make_async_remote_copy(

time: 30.8 us -> 30.8 us (level)
  no operation moved by 1% of the time
where the time goes in v6:
time: 30.8 us; the launch traced here: 30.6 us
  Pallas kernels  30 us (97%)
  between operations  0.64 us (2%)
    pallas_call x1, Pallas kernels, local(): pl.pallas_call(functools.partial(kernel, nx, ny, own), out_shape=out_shap...  28 us
    pallas_call x1, Pallas kernels, local(): pl.pallas_call(hand_over, out_shape=out_shape, in_specs=[hbm] * 3, out_sp...  1.99 us

profile of v6, /device:TPU:0, one launch (start us, length us, event | category | flops | bytes accessed | tf_op | source)
XLA Modules:
  0.0 30.6 jit_solution(4241621769254885988)
XLA Ops:
  0.6 28.0 %slab.1 = (f32[3,8,16,256]{3,2,1,0:T(8,128)}, f32[3,8,16,256]{3,2,1,0:T(8,128)}, f32[32,256]{1,0:T(8,128)}) custom-call(f32[3,8,16,256]{3,2,1,0:T(8,128)} %te_at.1, f32[3,8,16,256]{3,2,1,0:T(8,128)} %th_at.1, f32[3,8,4,16]{3,2,1,0:T(4,128)} %bitcast.5, f32[3,8,4,16]{3,2,1,0:T(4,128)} %bitcast.6, s32[8,4,16]{2,1,0:T(4,128)} %bitcast.7, s32[8,4,16]{2,1,0:T(4,128)} %bitcast.8, ...), custom_call_target="tpu_custom_call" | custom-call | tf_op jit(solution)/shard_map/slab/pallas_call | solution.py:420
  28.7 2.0 %hand_over.1 = (f32[3,8,16,256]{3,2,1,0:T(8,128)}, f32[3,8,16,256]{3,2,1,0:T(8,128)}, f32[32,256]{1,0:T(8,128)}) custom-call(f32[3,8,16,256]{3,2,1,0:T(8,128)} %get-tuple-element.6.from_e, f32[3,8,16,256]{3,2,1,0:T(8,128)} %get-tuple-element.7.from_h, f32[32,256]{1,0:T(8,128)} %get-tuple-element.8.from_s), custom_call_target="tpu_custom_call" | custom-call | tf_op jit(solution)/shard_map/hand_over/pallas_call | solution.py:447
